TPU v7x, 512 devices: a whole 4x8x8 slice. The times are simulated.
512 devices in a mesh: rows: 64 (over z, y), feat: 8 (over x, core).
Axes of the slice: x: 4, y: 8, z: 8, core: 2. Of those that a mesh axis runs over, the one named last changes fastest.
Arguments:
- bin_ids: int32 [512, 131072], P('feat', 'rows'), may hold values from 0 to 255
- leaf_ids: int32 [131072], P('rows'), may hold values from 0 to 63
- gradient: float32 [131072], P('rows'), may hold values from -6 to 6
- hessian: float32 [131072], P('rows'), may hold values from 0.01 to 0.25
- raw_feats: bfloat16 [131072, 64], P(('rows', 'feat')), may hold values from -6 to 6
- prior_score: float32 [131072], P(('rows', 'feat')), may hold values from -6 to 6
- elected: int32 [64, 64], P(None, 'feat'), may hold values from 0 to 63, as said below
Outputs:
- relative_gain: float32 [64, 64, 256], P('rows', 'feat')
- coefficients: float32 [64, 65], P('rows')
- new_score: float32 [131072], P(('rows', 'feat'))
Inputs may be any that keep to these rules, and one draw needn't show every extreme that they name: `elected`: within each row, each group's 8 entries are distinct feature numbers of that group.
All inputs are finite; a program needn't handle non-finite values.
Results may differ from a plain program's by a relative error of at most 0.0029.
Values sent between devices are 32-bit elements; how exact they have to be, the bound alone decides.
A program may use at most 64 MiB of HBM per device.

v0:
```python
import jax
import jax.numpy as jnp
from jax import lax
from jax.sharding import PartitionSpec as P

BINS = 256
SPLIT_REG = 1.0
RIDGE_REG = 1.0
SHRINKAGE = 0.3


def split_gains(hist_grad, hist_hess):
    left_grad = jnp.cumsum(hist_grad, axis=-1)
    left_hess = jnp.cumsum(hist_hess, axis=-1)
    total_grad = left_grad[..., -1:]
    total_hess = left_hess[..., -1:]
    right_grad = total_grad - left_grad
    first = left_grad * left_grad / (left_hess + SPLIT_REG)
    second = right_grad * right_grad / (total_hess - left_hess + SPLIT_REG)
    whole = total_grad * total_grad / (total_hess + SPLIT_REG)
    return first + second - whole


def solve_leaves(blocks):
    width = blocks.shape[2]
    system = blocks[:, :width, :] + RIDGE_REG * jnp.eye(width, dtype=blocks.dtype)
    target = blocks[:, width:, :]
    factor = jnp.linalg.cholesky(system)
    middle = lax.linalg.triangular_solve(
        factor, target, left_side=False, lower=True, transpose_a=True
    )
    answer = lax.linalg.triangular_solve(
        factor, middle, left_side=False, lower=True, transpose_a=False
    )
    return -answer[:, 0, :]


def body(bin_ids, leaf_ids, gradient, hessian, raw_feats, prior_score, elected):
    row_total = bin_ids.shape[1]
    leaf_total = elected.shape[0]
    slot_count = elected.shape[1]
    owned = leaf_total // lax.axis_size("rows")
    group_rows = row_total // lax.axis_size("feat")
    grad_round = gradient.astype(jnp.bfloat16)
    hess_round = hessian.astype(jnp.bfloat16)
    zero_value = jnp.zeros((), jnp.bfloat16)
    leaf_table = jnp.arange(leaf_total, dtype=jnp.int32)
    leaf_onehot = (leaf_ids[:, None] == leaf_table[None, :]).astype(jnp.float32)
    elected_cols = jnp.transpose(elected).astype(jnp.float32)
    picked = lax.dot_general(
        elected_cols, leaf_onehot, (((1,), (1,)), ((), ())), precision=lax.Precision.HIGHEST
    ).astype(jnp.int32)
    chosen = jnp.take_along_axis(bin_ids, picked, axis=0)
    bin_table = jnp.arange(BINS, dtype=jnp.int32)
    bin_onehot = (chosen[:, :, None] == bin_table[None, None, :]).astype(jnp.bfloat16)
    wanted = lax.broadcasted_iota(jnp.int32, (1, owned * lax.axis_size("rows")), 1)
    member = leaf_ids[:, None] == wanted
    grad_part = jnp.where(member, grad_round[:, None], zero_value)
    hess_part = jnp.where(member, hess_round[:, None], zero_value)
    weights = jnp.stack([grad_part, hess_part], axis=2).reshape(
        row_total, 2 * (owned * lax.axis_size("rows"))
    )
    product = lax.dot_general(
        weights, bin_onehot, (((0,), (1,)), ((), ())), preferred_element_type=jnp.float32
    )
    histogram = lax.psum_scatter(
        product.reshape(owned * lax.axis_size("rows"), 2, slot_count * BINS),
        "rows",
        scatter_dimension=0,
        tiled=True,
    )
    shaped = histogram.reshape(owned, 2, slot_count, BINS)
    gains = split_gains(shaped[:, 0], shaped[:, 1])
    local_best = jnp.max(gains, axis=(1, 2))
    best = lax.pmax(local_best, "feat")
    relative_gain = gains - best[:, None, None]
    group_start = lax.axis_index("feat") * group_rows
    leaf_sub = lax.dynamic_slice_in_dim(leaf_ids, group_start, group_rows)
    grad_sub = lax.dynamic_slice_in_dim(grad_round, group_start, group_rows)
    hess_sub = lax.dynamic_slice_in_dim(hessian, group_start, group_rows)
    unit_column = jnp.ones((group_rows, 1), jnp.bfloat16)
    augmented = jnp.concatenate([raw_feats, unit_column], axis=1)
    weighted = (hess_sub[:, None] * augmented.astype(jnp.float32)).astype(jnp.bfloat16)
    extended = jnp.concatenate([weighted, grad_sub[:, None]], axis=1)
    ext_width = extended.shape[1]
    wanted = lax.broadcasted_iota(jnp.int32, (1, owned * lax.axis_size("rows")), 1)
    member = leaf_sub[:, None] == wanted
    spread = jnp.where(member[:, :, None], extended[:, None, :], zero_value).reshape(
        group_rows, owned * lax.axis_size("rows") * ext_width
    )
    product = lax.dot_general(
        spread, augmented, (((0,), (0,)), ((), ())), preferred_element_type=jnp.float32
    )
    partial_blocks = lax.psum_scatter(
        product.reshape(owned * lax.axis_size("rows"), ext_width, ext_width - 1),
        "rows",
        scatter_dimension=0,
        tiled=True,
    )
    local_blocks = lax.psum(partial_blocks, "feat")
    coefficients = solve_leaves(local_blocks)
    all_coefs = lax.all_gather(coefficients, "rows", axis=0, tiled=True)
    sub_onehot = (leaf_sub[:, None] == leaf_table[None, :]).astype(jnp.float32)
    row_coefs = jnp.dot(sub_onehot, all_coefs, precision=lax.Precision.HIGHEST)
    new_score = prior_score + SHRINKAGE * jnp.sum(augmented.astype(jnp.float32) * row_coefs, axis=1)
    return (relative_gain, coefficients, new_score)


def solution(mesh):
    in_specs = (
        P("feat", "rows"),
        P("rows"),
        P("rows"),
        P("rows"),
        P(("rows", "feat"), None),
        P(("rows", "feat")),
        P(None, "feat"),
    )
    out_specs = (P("rows", "feat", None), P("rows", None), P(("rows", "feat")))
    return jax.shard_map(body, mesh=mesh, in_specs=in_specs, out_specs=out_specs, check_vma=False)
```

profile of v0, /device:TPU:2, one launch (start us, length us, event | category | flops | bytes accessed | tf_op | source)
XLA Modules:
  0.0 885.3 jit_solution(8825843172253596968)
XLA Ops:
  7.2 0.0 copy-start
  7.2 0.0 all-reduce.6.cloned.1.call-start
  7.2 0.7 convert_element_type.36
  8.0 0.7 convert_element_type.37
  8.7 1.6 compare_select_fusion.2
  10.4 0.0 copy-done
  10.4 0.0 copy-start.2
  10.4 130.6 %gather_fusion = s32[16384]{0:T(1024)S(1)} fusion(s32[64,2048]{1,0:T(8,128)S(1)} %copy-done, s32[16384]{0:T(1024)S(1)} %bitcast.78), kind=kCustom, calls=%fused_computation | custom fusion | bytes 262144 | tf_op jit(solution)/shard_map/jit(take_along_axis)/gather | solution.py:53
  141.0 0.0 copy-done.2
  141.0 0.8 compare_select_fusion.1
  141.8 1.2 pad_maximum_fusion
  143.0 0.2 reshape.597
  143.2 0.3 dot_general.21
  143.6 2.2 iota_compare_fusion
  145.8 0.0 copy-start.1
  145.8 3.0 fusion.3
  148.8 1.8 copy.14
  150.6 0.0 all-reduce.6.cloned.1.call-update
  150.6 0.0 reduce-scatter.4.cloned.1.call-start
  150.7 0.8 dynamic_slice.10
  151.4 0.0 copy-done.1
  151.4 0.1 dynamic_slice.9
  151.5 0.1 dynamic_slice.11
  151.6 0.2 broadcast_select_fusion
  151.8 2.1 select_n.54
  153.9 2.6 dot_general.25
  156.5 0.0 copy-start.5
  156.6 0.0 copy-start.3
  156.6 2.2 fusion.12
  158.7 0.0 reduce-scatter.4.cloned.1.call-update
  158.8 0.0 copy-done.5
  158.8 0.6 fusion.18
  160.0 156.6 %all-reduce.6.cloned.1.call-done = f32[64,2,2048]{2,1,0:T(2,128)} async-done(((f32[64,2,2048]{2,1,0:T(2,128)}), f32[64,2,2048]{2,1,0:T(2,128)}) %all-reduce.6.cloned.1.call-update) | async-done | bytes 1048592
  316.7 1.4 constant_dynamic-slice_fusion
  318.0 0.6 reduce-window.16
  318.6 0.2 slice_reduce_fusion
  318.8 0.6 reduce-window.14
  319.4 0.2 slice_reduce_fusion.1
  319.6 0.1 bitcast_add_fusion.1
  319.6 0.2 slice_reduce_fusion.3
  319.9 0.7 fusion.17
  320.5 10.6 %pmax.7 = f32[]{:T(128)} all-reduce(f32[]{:T(128)} %get-tuple-element.6), channel_id=1, replica_groups=mesh['rows'=64,'feat'=8] {'feat'}, use_global_device_ids=true, to_apply=%region_6.7 | all-reduce | flops 1 | bytes 8 | tf_op jit(solution)/shard_map/pmax | solution.py:75
  331.2 1.2 broadcast_subtract_fusion
  332.4 233.7 %reduce-scatter.4.cloned.1.call-done = f32[1,66,65]{2,1,0:T(8,128)} async-done(((f32[64,66,65]{2,1,0:T(8,128)}), f32[1,66,65]{2,1,0:T(8,128)}) %reduce-scatter.4.cloned.1.call-update) | async-done | bytes 17176
  566.1 21.7 %psum.7 = f32[1,66,65]{2,1,0:T(8,128)S(1)} all-reduce(f32[1,66,65]{2,1,0:T(8,128)} %reduce-scatter.4.cloned.1.call-done), channel_id=1, replica_groups=mesh['rows'=64,'feat'=8] {'feat'}, use_global_device_ids=true, to_apply=%region_8.9 | all-reduce | flops 4290 | bytes 34320 | tf_op jit(solution)/shard_map/psum | solution.py:100
  587.8 0.1 copy.15
  587.9 5.9 custom-call.9
  593.9 0.6 compare_reduce_fusion
  594.6 0.7 fusion.8
  595.2 5.0 custom-call.10
  600.2 0.1 convolution_bitcast_fusion.1
  600.4 0.2 fusion.2
  600.5 0.0 copy-start.4
  600.6 0.3 dynamic-update-slice.3
  600.8 276.6 %all-reduce.1 = f32[4160]{0:T(1024)S(1)} all-reduce(f32[4160]{0:T(1024)S(1)} %dynamic-update-slice.3), channel_id=2, replica_groups=mesh['rows'=64,'feat'=8] {'rows'}, use_global_device_ids=true, to_apply=%add.1 | all-reduce | flops 4160 | bytes 33280
  877.5 0.1 reshape.619
  877.6 0.2 fusion.1
  877.8 0.0 copy-done.3
  877.9 0.6 multiply_add_fusion
  878.4 0.0 copy-done.4
  (18 shorter events, 0.3 us)
Async XLA Ops:
  7.2 3.2 copy-start
  7.2 309.5 %all-reduce.6.cloned.1.call-start = ((), (), s32[]{:S(2)}) async-start(), calls=%async_computation.1 | async-start | bytes 2097152
  10.4 130.6 %copy-start.2 = (s32[2048]{0:T(1024)S(1)}, s32[2048]{0:T(1024)}, u32[]{:S(2)}) copy-start(s32[2048]{0:T(1024)} %param.8) | copy-start | bytes 24580
  145.8 5.7 copy-start.1
  150.6 415.5 %reduce-scatter.4.cloned.1.call-start = ((), (), s32[]{:S(2)}) async-start(), calls=%async_computation.2 | async-start | bytes 2396160
  156.5 2.2 copy-start.5
  156.6 721.3 %copy-start.3 = (f32[256]{0:T(256)S(1)}, f32[256]{0:T(256)}, u32[]{:S(2)}) copy-start(f32[256]{0:T(256)} %param.12) | copy-start | bytes 3076
  600.5 277.9 %copy-start.4 = (f32[65]{0:T(128)}, f32[65]{0:T(128)S(1)}, u32[]{:S(2)}) copy-start(f32[65]{0:T(128)S(1)} %fusion.2) | copy-start | bytes 784
Sparse Core Ops, SparseCore 0:
  150.7 165.8 all-reduce.5
  320.7 245.3 reduce-scatter.3
where the time goes:
time: 886 us; the launch traced here: 885 us
  waiting for transfers between devices  390 us (44%)
  blocking collectives  309 us (35%)
  local copies, waits for them, and re-layouts  141 us (16%)
  other arithmetic  22.2 us (3%)
  between operations  15 us (2%)
    unnamed x4, waiting for transfers between devices  390 us
    unnamed x1, blocking collectives  277 us
    gather x2, local copies, waits for them, and re-layouts, body(): chosen = jnp.take_along_axis(bin_ids, picked, axis=0)  131 us
    psum x1, blocking collectives, body(): local_blocks = lax.psum(partial_blocks, 'feat')  21.7 us
  transfers between devices with their start and end apart: 2, of which 2 were waited for; matrix products, arithmetic and copies ran while one was open for 2% of the time, Pallas kernels for 0%

commit v1 on v0

--- a/solution.py
+++ b/solution.py
@@ -97,7 +97,13 @@
         scatter_dimension=0,
         tiled=True,
     )
-    local_blocks = lax.psum(partial_blocks, "feat")
+    size = lax.axis_size("feat")
+    local_blocks, far = (partial_blocks, 1)
+    while far < size:
+        local_blocks = local_blocks + lax.ppermute(
+            local_blocks, "feat", [(i, i ^ far) for i in range(size)]
+        )
+        far = 2 * far
     coefficients = solve_leaves(local_blocks)
     all_coefs = lax.all_gather(coefficients, "rows", axis=0, tiled=True)
     sub_onehot = (leaf_sub[:, None] == leaf_table[None, :]).astype(jnp.float32)

time: 886 us -> 891 us (level)
  blocking collectives: 309 us -> 289 us
  waiting for transfers between devices: 390 us -> 407 us
    psum x1 -> x0, blocking collectives: 21.7 us -> none  [body(): local_blocks = lax.psum(partial_blocks, 'feat')]
    unnamed x4, waiting for transfers between devices: 390 us -> 403 us
  transfers between devices with their start and end apart: 2 -> 5, of which waited for: 2 -> 4; matrix products, arithmetic and copies ran while one was open for 2% -> 2% of each run, Pallas kernels for 0% -> 0%
where the time goes in v1:
time: 891 us
  waiting for transfers between devices  407 us (46%)
  blocking collectives  289 us (32%)
  local copies, waits for them, and re-layouts  141 us (16%)
  other arithmetic  22.9 us (3%)
  between operations  15 us (2%)
    unnamed x4, waiting for transfers between devices  403 us
    unnamed x1, blocking collectives  277 us
    gather x2, local copies, waits for them, and re-layouts, body(): chosen = jnp.take_along_axis(bin_ids, picked, axis=0)  131 us
  transfers between devices with their start and end apart: 5, of which 4 were waited for; matrix products, arithmetic and copies ran while one was open for 2% of the time, Pallas kernels for 0%

profile of v1, /device:TPU:2, one launch (start us, length us, event | category | flops | bytes accessed | tf_op | source)
XLA Modules:
  0.0 890.8 jit_solution(15174543272794571341)
XLA Ops:
  7.2 0.0 copy-start
  7.2 0.0 all-reduce.6.cloned.1.call-start
  7.2 0.7 convert_element_type.36
  8.0 0.7 convert_element_type.37
  8.7 1.6 compare_select_fusion.2
  10.4 0.0 copy-done
  10.4 0.0 copy-start.2
  10.4 130.6 %gather_fusion = s32[16384]{0:T(1024)S(1)} fusion(s32[64,2048]{1,0:T(8,128)S(1)} %copy-done, s32[16384]{0:T(1024)S(1)} %bitcast.78), kind=kCustom, calls=%fused_computation | custom fusion | bytes 262144 | tf_op jit(solution)/shard_map/jit(take_along_axis)/gather | solution.py:53
  141.0 0.0 copy-done.2
  141.0 0.8 compare_select_fusion.1
  141.8 1.2 pad_maximum_fusion
  143.0 0.2 reshape.597
  143.2 0.3 dot_general.21
  143.6 2.2 iota_compare_fusion
  145.8 0.0 copy-start.1
  145.8 3.0 fusion.3
  148.8 1.8 copy.14
  150.6 0.0 all-reduce.6.cloned.1.call-update
  150.6 0.0 reduce-scatter.4.cloned.1.call-start
  150.7 0.8 dynamic_slice.10
  151.4 0.0 copy-done.1
  151.4 0.1 dynamic_slice.9
  151.5 0.1 dynamic_slice.11
  151.6 0.2 broadcast_select_fusion
  151.8 2.1 select_n.54
  153.9 2.6 dot_general.25
  156.5 0.0 copy-start.5
  156.6 0.0 copy-start.3
  156.6 2.2 fusion.12
  158.7 0.0 reduce-scatter.4.cloned.1.call-update
  158.8 0.0 copy-done.5
  158.8 0.6 fusion.18
  160.0 156.6 %all-reduce.6.cloned.1.call-done = f32[64,2,2048]{2,1,0:T(2,128)} async-done(((f32[64,2,2048]{2,1,0:T(2,128)}), f32[64,2,2048]{2,1,0:T(2,128)}) %all-reduce.6.cloned.1.call-update) | async-done | bytes 1048592
  316.7 1.4 constant_dynamic-slice_fusion
  318.0 0.6 reduce-window.16
  318.6 0.2 slice_reduce_fusion
  318.8 0.6 reduce-window.14
  319.4 0.2 slice_reduce_fusion.1
  319.6 0.1 bitcast_add_fusion.1
  319.6 246.5 %reduce-scatter.4.cloned.1.call-done = f32[1,66,65]{2,1,0:T(8,128)} async-done(((f32[64,66,65]{2,1,0:T(8,128)}), f32[1,66,65]{2,1,0:T(8,128)}) %reduce-scatter.4.cloned.1.call-update) | async-done | bytes 17176
  566.1 1.9 collective-permute-start
  568.1 0.2 slice_reduce_fusion.3
  568.3 1.2 collective-permute-done
  569.4 0.8 add.102
  570.2 2.5 collective-permute-start.1
  572.7 0.7 fusion.17
  573.4 12.6 %pmax.7 = f32[]{:T(128)} all-reduce(f32[]{:T(128)} %get-tuple-element.6), channel_id=1, replica_groups=mesh['rows'=64,'feat'=8] {'feat'}, use_global_device_ids=true, to_apply=%region_6.7 | all-reduce | flops 1 | bytes 8 | tf_op jit(solution)/shard_map/pmax | solution.py:75
  585.9 0.0 collective-permute-done.1
  586.0 3.4 collective-permute-start.2
  589.3 1.2 broadcast_subtract_fusion
  590.6 2.7 collective-permute-done.2
  593.3 0.1 copy.15
  593.5 5.9 custom-call.9
  599.4 0.6 compare_reduce_fusion
  600.1 0.7 fusion.8
  600.7 5.0 custom-call.10
  605.7 0.1 convolution_bitcast_fusion.1
  605.9 0.2 fusion.2
  606.1 0.3 dynamic-update-slice.3
  606.3 276.6 %all-reduce.1 = f32[4160]{0:T(1024)S(1)} all-reduce(f32[4160]{0:T(1024)S(1)} %dynamic-update-slice.3), channel_id=2, replica_groups=mesh['rows'=64,'feat'=8] {'rows'}, use_global_device_ids=true, to_apply=%add.1 | all-reduce | flops 4160 | bytes 33280
  882.9 0.1 reshape.619
  883.1 0.2 fusion.1
  883.3 0.0 copy-done.3
  883.3 0.6 multiply_add_fusion
  (22 shorter events, 0.3 us)
Async XLA Ops:
  7.2 3.2 copy-start
  7.2 309.5 %all-reduce.6.cloned.1.call-start = ((), (), s32[]{:S(2)}) async-start(), calls=%async_computation.1 | async-start | bytes 2097152
  10.4 130.6 %copy-start.2 = (s32[2048]{0:T(1024)S(1)}, s32[2048]{0:T(1024)}, u32[]{:S(2)}) copy-start(s32[2048]{0:T(1024)} %param.8) | copy-start | bytes 24580
  145.8 5.7 copy-start.1
  150.6 415.5 %reduce-scatter.4.cloned.1.call-start = ((), (), s32[]{:S(2)}) async-start(), calls=%async_computation.2 | async-start | bytes 2396160
  156.5 2.2 copy-start.5
  156.6 726.8 %copy-start.3 = (f32[256]{0:T(256)S(1)}, f32[256]{0:T(256)}, u32[]{:S(2)}) copy-start(f32[256]{0:T(256)} %param.12) | copy-start | bytes 3076
  566.1 3.3 collective-permute-start
  570.2 15.7 %collective-permute-start.1 = (f32[1,66,65]{2,1,0:T(8,128)S(1)}, f32[1,66,65]{2,1,0:T(8,128)S(1)}, u32[]{:S(2)}, u32[]{:S(2)}) collective-permute-start(f32[1,66,65]{2,1,0:T(8,128)S(1)} %add.102), channel_id=1, source_target_pairs={{0,2},{1,3},{2,0},{3,1},{4,6},{5,7},{6,4},{7,5},{8,10},{9,11},{10,... | collective-permute-start | bytes 51488 | tf_op jit(solution)/shard_map/ppermute | solution.py:103
  586.0 7.4 collective-permute-start.2
  606.0 277.9 %copy-start.4 = (f32[65]{0:T(128)}, f32[65]{0:T(128)S(1)}, u32[]{:S(2)}) copy-start(f32[65]{0:T(128)S(1)} %fusion.2) | copy-start | bytes 784
Sparse Core Ops, SparseCore 0:
  150.7 165.8 all-reduce.5
  320.7 245.3 reduce-scatter.3
